TPU v7x, 32 devices: a whole 2x2x4 slice. The times are simulated.
32 devices in a mesh: dp: 8 (over y, x, core), tensor: 4 (over z).
Axes of the slice: x: 2, y: 2, z: 4, core: 2. Of those that a mesh axis runs over, the one named last changes fastest.
Arguments:
- tokens: bfloat16 [16384, 2048], P(('dp', 'tensor'))
- teacher: bfloat16 [16384, 2048], P(('dp', 'tensor')), may hold values from -6 to 6
- valid: int32 [16384], P(('dp', 'tensor')), may hold values from 0 to 1, as said below
- prefix: int32 [16], P('dp'), may hold values from 102 to 512, as said below
- w_query: bfloat16 [2048, 1024], P(None, 'tensor'), may hold values from -0.125 to 0.125
- key_weight: bfloat16 [2048, 256], replicated, may hold values from -0.125 to 0.125
- value_weight: bfloat16 [2048, 256], replicated, may hold values from -0.125 to 0.125
- query_gain: float32 [64], replicated, may hold values from 0.25 to 1.75
- key_gain: float32 [64], replicated, may hold values from 0.25 to 1.75
- w_out: bfloat16 [1024, 2048], P('tensor'), may hold values from -3 to 3
- attn_gain: float32 [2048], replicated, may hold values from 0.25 to 1.75
- ffn_gain: float32 [2048], replicated, may hold values from 0.25 to 1.75
- w_gate: bfloat16 [2048, 5120], P(None, 'tensor'), may hold values from -0.125 to 0.125
- w_up: bfloat16 [2048, 5120], P(None, 'tensor'), may hold values from -0.125 to 0.125
- w_down: bfloat16 [5120, 2048], P('tensor'), may hold values from -0.078125 to 0.078125
Outputs:
- output: bfloat16 [16384, 2048], P(('dp', 'tensor'))
- loss: float32 [], replicated
- grad_tokens: float32 [16384, 2048], P(('dp', 'tensor'))
- grad_query: float32 [2048, 1024], P(None, 'tensor')
- grad_key: float32 [2048, 256], replicated
- grad_value: float32 [2048, 256], replicated
- grad_query_gain: float32 [64], replicated
- grad_key_gain: float32 [64], replicated
- grad_out: float32 [1024, 2048], P('tensor')
- grad_attn_gain: float32 [2048], replicated
- grad_ffn_gain: float32 [2048], replicated
- grad_gate: float32 [2048, 5120], P(None, 'tensor')
- grad_up: float32 [2048, 5120], P(None, 'tensor')
- grad_down: float32 [5120, 2048], P('tensor')
Inputs may be any that keep to these rules, and one draw needn't show every extreme that they name: The first token of every sequence is valid. One sequence has prefix length exactly 512 and another exactly 102.
All inputs are finite; a program needn't handle non-finite values.
Results may differ from a plain program's by a relative error of at most 0.015.
Values may be sent and summed in bfloat16 or wider, within the bound.
A program may use at most 256 MiB of HBM per device.

v0:
```python
import jax
import jax.numpy as jnp
from jax import lax
from jax.sharding import PartitionSpec as P

QUERY_HEADS = 16
KEY_VALUE_HEADS = 4
HEAD_SIZE = 64
SEQ_LEN = 1024
GROUP = QUERY_HEADS // KEY_VALUE_HEADS
EPSILON = 1e-06
BF = jnp.bfloat16
F32 = jnp.float32


def rope_rows(start, rows):
    half = HEAD_SIZE // 2
    frequency = 10000.0 ** (-2.0 * jnp.arange(half, dtype=F32) / HEAD_SIZE)
    angles = (start + jnp.arange(rows)).astype(F32)[:, None] * frequency[None, :]
    cosine = jnp.concatenate([jnp.cos(angles), jnp.cos(angles)], 1)
    sine = jnp.concatenate([jnp.sin(angles), jnp.sin(angles)], 1)
    return (cosine[:, None, :], sine[:, None, :])


def rotate(vector, cosine, sine):
    half = vector.shape[-1] // 2
    turned = jnp.concatenate([-vector[..., half:], vector[..., :half]], -1)
    return vector * cosine + turned * sine


def unrotate(gradient, cosine, sine):
    half = gradient.shape[-1] // 2
    shifted = gradient * sine
    return gradient * cosine + jnp.concatenate([shifted[..., half:], -shifted[..., :half]], -1)


def inv_root(vector):
    return lax.rsqrt(jnp.mean(vector * vector, axis=-1, keepdims=True) + EPSILON)


def norm_back(gradient, source, factor, gain):
    scaled = gradient * gain
    return factor * scaled - source * factor**3 * jnp.mean(scaled * source, axis=-1, keepdims=True)


def dot(a, b):
    return jnp.dot(a, b, preferred_element_type=F32)


def dot_t(a, b):
    return lax.dot_general(a, b, (((1,), (1,)), ((), ())), preferred_element_type=F32)


def t_dot(a, b):
    return lax.dot_general(a, b, (((0,), (0,)), ((), ())), preferred_element_type=F32)


def seen(start, rows, prefix_len):
    row = start + jnp.arange(rows)[:, None]
    col = jnp.arange(SEQ_LEN)[None, :]
    return (col <= row) | (row < prefix_len) & (col < prefix_len)


def attend(q, k, v, start, prefix_len):
    rows = q.shape[0]
    grouped = q.reshape(rows, KEY_VALUE_HEADS, GROUP, HEAD_SIZE)
    scores = jnp.einsum("ikgd,jkd->kgij", grouped, k, preferred_element_type=F32) * HEAD_SIZE ** (
        -0.5
    )
    allowed = seen(start, rows, prefix_len)
    scores = jnp.where(allowed, scores, -1e30)
    top = jnp.max(scores, -1, keepdims=True)
    weights = jnp.where(allowed, jnp.exp(scores - top), 0.0)
    total = jnp.sum(weights, -1, keepdims=True)
    probs = (weights / total).astype(BF)
    attended = jnp.einsum("kgij,jkd->ikgd", probs, v, preferred_element_type=F32)
    return (attended.reshape(rows, QUERY_HEADS * HEAD_SIZE), (top + jnp.log(total))[..., 0])


def attend_back(q, k, v, start, prefix_len, lse, grad):
    rows = q.shape[0]
    scale = HEAD_SIZE ** (-0.5)
    grouped = q.reshape(rows, KEY_VALUE_HEADS, GROUP, HEAD_SIZE)
    scores = jnp.einsum("ikgd,jkd->kgij", grouped, k, preferred_element_type=F32) * scale
    allowed = seen(start, rows, prefix_len)
    probs = jnp.where(allowed, jnp.exp(jnp.where(allowed, scores, -1e30) - lse[..., None]), 0.0)
    heads = grad.reshape(rows, KEY_VALUE_HEADS, GROUP, HEAD_SIZE)
    dprobs = jnp.einsum("ikgd,jkd->kgij", heads, v, preferred_element_type=F32)
    inner = jnp.sum(probs * dprobs, -1, keepdims=True)
    dscores = (probs * (dprobs - inner)).astype(BF)
    dq = jnp.einsum("kgij,jkd->ikgd", dscores, k, preferred_element_type=F32) * scale
    dk = jnp.einsum("kgij,ikgd->jkd", dscores, grouped, preferred_element_type=F32) * scale
    dv = jnp.einsum("kgij,ikgd->jkd", probs.astype(BF), heads, preferred_element_type=F32)
    return (dq.reshape(rows, QUERY_HEADS, HEAD_SIZE), dk, dv)


def sum_small(vector):
    return jnp.sum(lax.all_gather(vector[None], ("dp", "tensor"), axis=0, tiled=True), 0)


def body(
    tokens,
    teacher,
    valid,
    prefix,
    w_query,
    key_weight,
    value_weight,
    query_gain,
    key_gain,
    w_out,
    attn_gain,
    ffn_gain,
    w_gate,
    w_up,
    w_down,
):
    rows, width = tokens.shape
    dp_size, t_size = (lax.axis_size("dp"), lax.axis_size("tensor"))
    dp_at, t_at = (lax.axis_index("dp"), lax.axis_index("tensor"))
    per_seq = SEQ_LEN // rows
    seq_groups = [list(range(g, g + per_seq)) for g in range(0, t_size, per_seq)]
    start = t_at % per_seq * rows
    prefix_len = prefix[t_at // per_seq]
    q_all = QUERY_HEADS * HEAD_SIZE
    kv_all = KEY_VALUE_HEADS * HEAD_SIZE
    q_dev = w_query.shape[1]
    cut = width // dp_size
    count = sum_small(jnp.broadcast_to(jnp.sum(valid).astype(F32), (128,)))[0]
    query_cut = lax.dynamic_slice_in_dim(w_query, dp_at * cut, cut, 0)
    query_full = (
        lax.all_gather(query_cut, ("dp", "tensor"), axis=0, tiled=False)
        .reshape(dp_size, t_size, cut, q_dev)
        .transpose(0, 2, 1, 3)
        .reshape(width, q_all)
    )
    out_rows = w_out.shape[0] // dp_size
    out_cut = lax.dynamic_slice_in_dim(w_out, dp_at * out_rows, out_rows, 0)
    out_full = lax.all_gather(out_cut, ("tensor", "dp"), axis=0, tiled=True)
    source = tokens.astype(F32)
    factor_one = inv_root(source)
    normed = (source * factor_one * attn_gain).astype(BF)
    k_raw = dot(normed, key_weight).reshape(rows, KEY_VALUE_HEADS, HEAD_SIZE)
    v_low = dot(normed, value_weight).astype(BF)
    cosine, sine = rope_rows(start, rows)
    k_factor = inv_root(k_raw)
    k_low = rotate(k_raw * k_factor * key_gain, cosine, sine).astype(BF).reshape(rows, kv_all)
    kv_seq = lax.all_gather(
        jnp.concatenate([k_low, v_low], 1),
        "tensor",
        axis=0,
        tiled=True,
        axis_index_groups=seq_groups,
    )
    k_seq = kv_seq[:, :kv_all].reshape(SEQ_LEN, KEY_VALUE_HEADS, HEAD_SIZE)
    v_seq = kv_seq[:, kv_all:].reshape(SEQ_LEN, KEY_VALUE_HEADS, HEAD_SIZE)
    q_raw = dot(normed, query_full).reshape(rows, QUERY_HEADS, HEAD_SIZE)
    q_factor = inv_root(q_raw)
    q_low = rotate(q_raw * q_factor * query_gain, cosine, sine).astype(BF)
    attended, lse = attend(q_low, k_seq, v_seq, start, prefix_len)
    attended = attended.astype(BF)
    middle = source + dot(attended, out_full)
    factor_two = inv_root(middle)
    normed_two = (middle * factor_two * ffn_gain).astype(BF)
    normed_two_all = lax.all_gather(normed_two, "tensor", axis=0, tiled=True)
    gate = dot(normed_two_all, w_gate)
    up = dot(normed_two_all, w_up)
    sig = jax.nn.sigmoid(gate)
    hidden = (gate * sig * up).astype(BF)
    result = middle + lax.psum_scatter(
        dot(hidden, w_down).astype(BF), "tensor", scatter_dimension=0, tiled=True
    ).astype(F32)
    mask = valid.astype(F32)[:, None]
    error = result - teacher.astype(F32)
    squares = jnp.sum(error * error * mask)
    cot = rows * t_size * dp_size / count * error * mask
    cot_all = lax.all_gather(cot.astype(BF), "tensor", axis=0, tiled=True)
    grad_down = t_dot(hidden, cot_all)
    dhidden = dot_t(cot_all, w_down)
    dgate = (dhidden * up * sig * (1.0 + gate * (1.0 - sig))).astype(BF)
    dup = (dhidden * gate * sig).astype(BF)
    dn2 = lax.psum_scatter(
        (dot_t(dgate, w_gate) + dot_t(dup, w_up)).astype(BF),
        "tensor",
        scatter_dimension=0,
        tiled=True,
    ).astype(F32)
    grad_gate = t_dot(normed_two_all, dgate)
    grad_up = t_dot(normed_two_all, dup)
    grad_gate, grad_up, grad_down = (
        lax.psum(g.astype(BF), "dp").astype(F32) for g in (grad_gate, grad_up, grad_down)
    )
    grad_ffn_gain = jnp.sum(dn2 * middle * factor_two, 0)
    dmiddle = cot + norm_back(dn2, middle, factor_two, ffn_gain)
    da = dmiddle.astype(BF)
    grad_out_t = t_dot(da, attended).astype(BF)
    dattended = dot_t(da, out_full).astype(BF)
    dq_rot, dk_part, dv_part = attend_back(q_low, k_seq, v_seq, start, prefix_len, lse, dattended)
    dkv = lax.psum_scatter(
        jnp.concatenate(
            [dk_part.reshape(SEQ_LEN, kv_all), dv_part.reshape(SEQ_LEN, kv_all)], 1
        ).astype(BF),
        "tensor",
        scatter_dimension=0,
        tiled=True,
        axis_index_groups=seq_groups,
    ).astype(F32)
    dq_normed = unrotate(dq_rot, cosine, sine)
    dk_normed = unrotate(dkv[:, :kv_all].reshape(rows, KEY_VALUE_HEADS, HEAD_SIZE), cosine, sine)
    grad_query_gain = jnp.sum(dq_normed * q_raw * q_factor, (0, 1))
    grad_key_gain = jnp.sum(dk_normed * k_raw * k_factor, (0, 1))
    dq = norm_back(dq_normed, q_raw, q_factor, query_gain).reshape(rows, q_all).astype(BF)
    dk = norm_back(dk_normed, k_raw, k_factor, key_gain).reshape(rows, kv_all).astype(BF)
    dv = dkv[:, kv_all:].astype(BF)
    dn1 = dot_t(dq, query_full) + dot_t(dk, key_weight) + dot_t(dv, value_weight)
    grad_attn_gain = jnp.sum(dn1 * source * factor_one, 0)
    grad_tokens = dmiddle + norm_back(dn1, source, factor_one, attn_gain)
    grad_query = t_dot(normed, dq).astype(BF)
    grad_kv = t_dot(normed, jnp.concatenate([dk, dv], 1)).astype(BF)
    wide = jnp.concatenate([grad_query, grad_out_t, grad_kv], 1)
    wide = lax.psum_scatter(wide, "dp", scatter_dimension=0, tiled=True)
    parts = jnp.concatenate(
        [
            wide[:, : 2 * q_all]
            .reshape(cut, 2, t_size, q_dev)
            .transpose(0, 2, 1, 3)
            .reshape(cut, t_size, 2 * q_dev),
            wide[:, 2 * q_all :].reshape(cut, t_size, 2 * kv_all // t_size),
        ],
        2,
    ).reshape(cut, -1)
    parts = lax.psum_scatter(parts, "tensor", scatter_dimension=1, tiled=True)
    own = lax.all_gather(parts[:, : 2 * q_dev], "dp", axis=0, tiled=True).astype(F32)
    grad_query = own[:, :q_dev]
    grad_out = own[:, q_dev:].T
    kv = (
        lax.all_gather(parts[:, 2 * q_dev :], ("dp", "tensor"), axis=0, tiled=False)
        .reshape(dp_size, t_size, cut, 2 * kv_all // t_size)
        .transpose(0, 2, 1, 3)
        .reshape(width, 2 * kv_all)
        .astype(F32)
    )
    small = sum_small(
        jnp.concatenate(
            [
                grad_attn_gain,
                grad_ffn_gain,
                grad_query_gain,
                grad_key_gain,
                jnp.broadcast_to(squares, (128,)),
            ]
        )
    )
    loss = small[2 * width + 2 * HEAD_SIZE] / (count * width)
    return (
        result.astype(BF),
        loss,
        grad_tokens,
        grad_query,
        kv[:, :kv_all],
        kv[:, kv_all:],
        small[2 * width : 2 * width + HEAD_SIZE],
        small[2 * width + HEAD_SIZE : 2 * width + 2 * HEAD_SIZE],
        grad_out,
        small[:width],
        small[width : 2 * width],
        grad_gate,
        grad_up,
        grad_down,
    )


def solution(mesh):
    rows, cols, whole = (P(("dp", "tensor"), None), P(None, "tensor"), P())
    down = P("tensor", None)
    return jax.shard_map(
        body,
        mesh=mesh,
        in_specs=(
            rows,
            rows,
            P(("dp", "tensor")),
            P("dp"),
            cols,
            whole,
            whole,
            whole,
            whole,
            down,
            whole,
            whole,
            cols,
            cols,
            down,
        ),
        out_specs=(
            rows,
            whole,
            rows,
            cols,
            whole,
            whole,
            whole,
            whole,
            down,
            whole,
            whole,
            cols,
            cols,
            down,
        ),
        check_vma=False,
    )
```

profile of v0, /device:TPU:0, one launch (start us, length us, event | category | flops | bytes accessed | tf_op | source)
XLA Modules:
  0.0 1515.2 jit_solution(16040654577957878719)
XLA Ops:
  23.7 17.6 %all-gather.12.cloned.1.call-done = bf16[1024,512]{0,1:T(8,128)(2,1)} async-done(((bf16[512,512]{0,1:T(8,128)(2,1)}), bf16[1024,512]{0,1:T(8,128)(2,1)}) %all-gather.12.cloned.1.call-update) | async-done | bytes 1048592 | tf_op jit(solution)/shard_map/all_gather | solution.py:148
  43.6 63.4 %all-gather.22.cloned.1.call-done = bf16[8192,256]{1,0:T(8,128)(2,1)} async-done(((bf16[256,256]{1,0:T(8,128)(2,1)}), bf16[8192,256]{1,0:T(8,128)(2,1)}) %all-gather.22.cloned.1.call-update) | async-done | bytes 4194320 | tf_op jit(solution)/shard_map/all_gather | solution.py:132
  153.1 16.4 %fusion.33 = bf16[4,64,4,512]{3,1,2,0:T(8,128)(2,1)} fusion(bf16[1024,4,64,1]{0,2,3,1:T(8,128)(2,1)S(1)} %bitcast.229, f32[4,4,512]{2,1,0:T(4,128)S(1)} %fusion.3, f32[4,4,512]{2,1,0:T(4,128)S(1)} %get-tuple-element.123, pred[512,1024]{0,1:T(8,128)(4,1)S(1)} %copy-done.10, f32[4,1024,512,4]{2,1,3,0:T(8,128)} %get-tuple-element.124), kind=kOutput, calls=%fused_computation.80 | convolution fusion | flops 1124597760 | bytes 35717120 | tf_op jit(solution)/shard_map/kgij,jkd->ikgd/dot_general | solution.py:76
  180.1 148.3 %all-gather.16.cloned.1.call-done = bf16[2048,2048]{1,0:T(8,128)(2,1)} async-done(((bf16[512,2048]{1,0:T(8,128)(2,1)}), bf16[2048,2048]{1,0:T(8,128)(2,1)}) %all-gather.16.cloned.1.call-update) | async-done | bytes 8388624 | tf_op jit(solution)/shard_map/all_gather | solution.py:165
  328.4 16.7 %fusion.78 = f32[2048,1280]{1,0:T(8,128)} fusion(bf16[2048,2048]{1,0:T(8,128)(2,1)} %all-gather.16.cloned.1.call-done, bf16[2048,1280]{1,0:T(8,128)(2,1)} %param.27), kind=kOutput, calls=%fused_computation.162 | convolution fusion | flops 10737418240 | bytes 24117248 | tf_op jit(solution)/shard_map/dot_general | solution.py:47
  345.0 17.3 %multiply_convert_fusion.2 = (bf16[2048,1280]{1,0:T(8,128)(2,1)}, f32[2048,1280]{1,0:T(8,128)}) fusion(f32[2048,1280]{1,0:T(8,128)} %fusion.78, bf16[2048,2048]{1,0:T(8,128)(2,1)S(1)} %copy-done.77, bf16[2048,1280]{1,0:T(8,128)(2,1)} %param.28), kind=kOutput, calls=%fused_computation.19 | convolution fusion | flops 10753146880 | bytes 39845888 | tf_op jit(solution)/shard_map/dot_general | solution.py:47
  362.3 16.6 %convolution_convert_fusion = bf16[2048,2048]{1,0:T(8,128)(2,1)} fusion(bf16[2048,1280]{1,0:T(8,128)(2,1)} %get-tuple-element.127, bf16[1280,2048]{1,0:T(8,128)(2,1)} %param.29), kind=kOutput, calls=%fused_computation.27 | convolution fusion | flops 10741612544 | bytes 18874368 | tf_op jit(solution)/shard_map/dot_general | solution.py:47
  381.0 42.9 %all-reduce = f32[32]{0:T(128)S(1)} all-reduce(f32[32]{0:T(128)S(1)} %dynamic-update-slice), channel_id=2, replica_groups=mesh['dp'=8,'tensor'=4] {'dp','tensor'}, use_global_device_ids=true, to_apply=%add | all-reduce | flops 32 | bytes 256
  424.1 98.7 %reduce-scatter.6.cloned.1.call-done = bf16[512,2048]{1,0:T(8,128)(2,1)} async-done(((bf16[2048,2048]{1,0:T(8,128)(2,1)}), bf16[512,2048]{1,0:T(8,128)(2,1)}) %reduce-scatter.6.cloned.1.call-update) | async-done | bytes 2097168 | tf_op jit(solution)/shard_map/reduce_scatter | solution.py:170
  528.2 150.4 %all-gather.18.cloned.1.call-done = bf16[2048,2048]{1,0:T(8,128)(2,1)} async-done(((bf16[512,2048]{1,0:T(8,128)(2,1)}), bf16[2048,2048]{1,0:T(8,128)(2,1)}) %all-gather.18.cloned.1.call-update) | async-done | bytes 8388624 | tf_op jit(solution)/shard_map/all_gather | solution.py:177
  678.7 24.3 %multiply_convert_fusion = (bf16[2048,1280]{1,0:T(8,128)(2,1)}, bf16[2048,1280]{1,0:T(8,128)(2,1)}) fusion(f32[2048,1280]{1,0:T(8,128)} %fusion.78, f32[2048,1280]{1,0:T(8,128)} %get-tuple-element.128, bf16[2048,2048]{1,0:T(8,128)(2,1)} %all-gather.18.cloned.1.call-done, bf16[1280,2048]{1,0:T(8,128)(2,1)} %param.29), kind=kOutput, calls=%fused_computation.17 | convolution fusion | flops 10771496960 | bytes 45088768 | tf_op jit(solution)/shard_map/dot_general | solution.py:51
  702.9 17.9 %fusion.79 = f32[2048,2048]{1,0:T(8,128)} fusion(bf16[2048,1280]{1,0:T(8,128)(2,1)} %get-tuple-element.82, bf16[2048,1280]{1,0:T(8,128)(2,1)} %param.27), kind=kOutput, calls=%fused_computation.163 | convolution fusion | flops 10737418240 | bytes 27262976 | tf_op jit(solution)/shard_map/dot_general | solution.py:51
  720.8 19.2 %add_convert_fusion = bf16[2048,2048]{1,0:T(8,128)(2,1)} fusion(f32[2048,2048]{1,0:T(8,128)} %fusion.79, bf16[2048,1280]{1,0:T(8,128)(2,1)} %get-tuple-element.81, bf16[2048,1280]{1,0:T(8,128)(2,1)} %param.28), kind=kOutput, calls=%fused_computation.11 | convolution fusion | flops 10745806848 | bytes 35651584 | tf_op jit(solution)/shard_map/dot_general | solution.py:51
  740.8 142.1 %reduce-scatter.8.cloned.1.call-done = bf16[512,2048]{1,0:T(8,128)(2,1)} async-done(((bf16[2048,2048]{1,0:T(8,128)(2,1)}), bf16[512,2048]{1,0:T(8,128)(2,1)}) %reduce-scatter.8.cloned.1.call-update) | async-done | bytes 2097168 | tf_op jit(solution)/shard_map/reduce_scatter | solution.py:182
  899.7 24.3 %fusion = (f32[4,4,512]{2,1,0:T(4,128)S(1)}, f32[4,1024,512,4]{2,1,3,0:T(8,128)}) fusion(f32[4,4,512]{2,1,0:T(4,128)S(1)} %bitcast.233, pred[512,1024]{0,1:T(8,128)(4,1)S(1)} %copy-done.11, f32[4,1024,512,4]{2,1,3,0:T(8,128)} %get-tuple-element.124, bf16[1024,4,64,1]{0,2,3,1:T(8,128)(2,1)S(1)} %bitcast.230, bf16[512,4,4,64]{0,3,2,1:T(8,128)(2,1)S(1)} %bitcast.227), kind=kOutput, calls=%fused_computation.2 | convolution fusion | flops 1124065280 | bytes 69271552 | tf_op jit(solution)/shard_map/ikgd,jkd->kgij/dot_general | solution.py:88
  924.0 16.1 %fusion.39 = bf16[4,64,1024]{2,1,0:T(8,128)(2,1)} fusion(bf16[512,4,4,64]{0,3,2,1:T(8,128)(2,1)S(1)} %bitcast.228, f32[4,4,512]{2,1,0:T(4,128)S(1)} %bitcast.234, pred[512,1024]{0,1:T(8,128)(4,1)S(1)} %copy-done.11, f32[4,1024,512,4]{2,1,3,0:T(8,128)} %get-tuple-element.124), kind=kOutput, calls=%fused_computation.86 | convolution fusion | flops 1115947008 | bytes 35684352 | tf_op jit(solution)/shard_map/kgij,ikgd->jkd/dot_general | solution.py:93
  940.2 28.0 %fusion.2 = bf16[4,4,512,1024]{2,3,1,0:T(8,128)(2,1)} fusion(f32[4,1024,512,4]{2,1,3,0:T(8,128)} %get-tuple-element.130, f32[4,4,512]{2,1,0:T(4,128)S(1)} %get-tuple-element.129, f32[4,4,512]{2,1,0:T(4,128)S(1)} %bitcast.235, pred[512,1024]{0,1:T(8,128)(4,1)S(1)} %copy-done.11, f32[4,1024,512,4]{2,1,3,0:T(8,128)} %get-tuple-element.124), kind=kLoop, calls=%fused_computation.4 | loop fusion | flops 58720256 | bytes 84475904 | tf_op jit(solution)/shard_map/convert_element_type | solution.py:90
  1018.6 18.0 %pad_maximum_fusion = bf16[2048,2560]{0,1:T(8,128)(2,1)} fusion(bf16[2048,512]{0,1:T(8,128)(2,1)S(1)} %convolution_convert_fusion.6, bf16[2048,1024]{0,1:T(8,128)(2,1)S(1)} %copy-done.34, bf16[2048,1024]{0,1:T(8,128)(2,1)S(1)} %copy-done.33), kind=kLoop, calls=%fused_computation.16 | loop fusion | flops 31457280 | bytes 20971520 | tf_op jit(solution)/shard_map/concatenate | solution.py:220
  1036.8 16.7 %convolution_convert_fusion.2 = bf16[2048,1280]{1,0:T(8,128)(2,1)} fusion(bf16[2048,2048]{1,0:T(8,128)(2,1)} %all-gather.16.cloned.1.call-done, bf16[2048,1280]{1,0:T(8,128)(2,1)} %get-tuple-element.81), kind=kOutput, calls=%fused_computation.29 | convolution fusion | flops 10740039680 | bytes 18874368 | tf_op jit(solution)/shard_map/dot_general | solution.py:55
  1053.5 17.0 %convolution_convert_fusion.3 = bf16[2048,1280]{1,0:T(8,128)(2,1)} fusion(bf16[2048,2048]{1,0:T(8,128)(2,1)} %all-gather.16.cloned.1.call-done, bf16[2048,1280]{1,0:T(8,128)(2,1)} %get-tuple-element.82), kind=kOutput, calls=%fused_computation.30 | convolution fusion | flops 10740039680 | bytes 18874368 | tf_op jit(solution)/shard_map/dot_general | solution.py:55
  1070.5 47.8 %reduce-scatter.12.cloned.1.call-done = bf16[256,2560]{0,1:T(8,128)(2,1)} async-done(((bf16[2048,2560]{0,1:T(8,128)(2,1)}), bf16[256,2560]{0,1:T(8,128)(2,1)}) %reduce-scatter.12.cloned.1.call-update) | async-done | bytes 1310736 | tf_op jit(solution)/shard_map/reduce_scatter | solution.py:221
  1121.2 16.6 %convolution_convert_fusion.1 = bf16[1280,2048]{1,0:T(8,128)(2,1)} fusion(bf16[2048,1280]{1,0:T(8,128)(2,1)} %get-tuple-element.127, bf16[2048,2048]{1,0:T(8,128)(2,1)} %all-gather.18.cloned.1.call-done), kind=kOutput, calls=%fused_computation.28 | convolution fusion | flops 10740039680 | bytes 18874368 | tf_op jit(solution)/shard_map/dot_general | solution.py:55
  1155.7 208.1 %all-reduce.4.cloned.1.call-done = (bf16[2048,1280]{1,0:T(8,128)(2,1)}, bf16[2048,1280]{1,0:T(8,128)(2,1)}, bf16[1280,2048]{1,0:T(8,128)(2,1)}) async-done(((bf16[2048,1280]{1,0:T(8,128)(2,1)}, bf16[2048,1280]{1,0:T(8,128)(2,1)}, bf16[1280,2048]{1,0:T(8,128)(2,1)}), (bf16[2048,1280]{1,0:T(8,128)(2,1)}, bf16[2048,1280]{1,0:T(8,128)(2,1)}, bf16[1280,2048]{1,0:T(8,128)(2,1)})) %all-reduce.4.cloned.1.call-update) | async-done | bytes 15728656 | tf_op jit(solution)/shard_map/psum | solution.py:191
  1393.7 78.0 %all-gather.3 = f32[32,1,4352]{2,1,0:T(1,128)} all-gather(f32[1,1,4352]{2,1,0:T(1,128)S(1)} %reshape.250), channel_id=4, replica_groups=mesh['dp'=8,'tensor'=4] {'dp','tensor'}, dimensions={0}, use_global_device_ids=true | all-gather | bytes 574464 | tf_op jit(solution)/shard_map/all_gather | solution.py:98
  (294 shorter events, 235.2 us)
Async XLA Ops:
  7.2 34.1 %all-gather.12.cloned.1.call-start = ((), (), s32[]{:S(2)}) async-start(), calls=%async_computation.5 | async-start | bytes 1572864 | tf_op jit(solution)/shard_map/all_gather | solution.py:148
  9.9 109.1 %copy-start.62 = (f32[512]{0:T(512)}, f32[512]{0:T(512)S(1)}, u32[]{:S(2)}) copy-start(f32[512]{0:T(512)S(1)} %get-tuple-element.114) | copy-start | bytes 6148
  16.0 107.0 %copy-start.30 = (f32[512,64]{0,1:T(8,128)}, f32[512,64]{0,1:T(8,128)S(1)}, u32[]{:S(2)}) copy-start(f32[512,64]{0,1:T(8,128)S(1)} %get-tuple-element.132) | copy-start | bytes 393220
  16.0 107.0 %copy-start.35 = (f32[512,64]{0,1:T(8,128)}, f32[512,64]{0,1:T(8,128)S(1)}, u32[]{:S(2)}) copy-start(f32[512,64]{0,1:T(8,128)S(1)} %get-tuple-element.133) | copy-start | bytes 393220
  17.1 89.8 %all-gather.22.cloned.1.call-start = ((), (), s32[]{:S(2)}) async-start(), calls=%async_computation.15 | async-start | bytes 4325376 | tf_op jit(solution)/shard_map/all_gather | solution.py:132
  18.8 152.3 %all-gather.14.cloned.1.call-start = ((), (), s32[]{:S(2)}) async-start(), calls=%async_computation.6 | async-start | bytes 4325376 | tf_op jit(solution)/shard_map/all_gather | solution.py:139
  20.4 307.9 %all-gather.16.cloned.1.call-start = ((), (), s32[]{:S(2)}) async-start(), calls=%async_computation.7 | async-start | bytes 10485760 | tf_op jit(solution)/shard_map/all_gather | solution.py:165
  180.0 342.7 %reduce-scatter.6.cloned.1.call-start = ((), (), s32[]{:S(2)}) async-start(), calls=%async_computation.8 | async-start | bytes 10485760 | tf_op jit(solution)/shard_map/reduce_scatter | solution.py:170
  378.9 143.9 %copy-start.13 = (bf16[512,2048]{1,0:T(8,128)(2,1)S(1)}, bf16[512,2048]{1,0:T(8,128)(2,1)}, u32[]{:S(2)}) copy-start(bf16[512,2048]{1,0:T(8,128)(2,1)} %param.16) | copy-start | bytes 6291460
  378.9 299.8 %all-gather.18.cloned.1.call-start = ((), (), s32[]{:S(2)}) async-start(), calls=%async_computation.9 | async-start | bytes 10485760 | tf_op jit(solution)/shard_map/all_gather | solution.py:177
  424.0 104.2 %copy-start.79 = (f32[128]{0:T(128)}, f32[128]{0:T(128)S(1)}, u32[]{:S(2)}) copy-start(f32[128]{0:T(128)S(1)} %broadcast_reduce_fusion) | copy-start | bytes 1540
  528.2 354.7 %reduce-scatter.8.cloned.1.call-start = ((), (), s32[]{:S(2)}) async-start(), calls=%async_computation.10 | async-start | bytes 10485760 | tf_op jit(solution)/shard_map/reduce_scatter | solution.py:182
  740.0 142.9 %copy-start.55 = (f32[2048]{0:T(1024)S(1)}, f32[2048]{0:T(1024)}, u32[]{:S(2)}) copy-start(f32[2048]{0:T(1024)} %param.26) | copy-start | bytes 24580
  740.0 142.9 %copy-start.61 = (f32[512]{0:T(512)S(1)}, f32[512]{0:T(512)}, u32[]{:S(2)}) copy-start(f32[512]{0:T(512)} %copy-done.60) | copy-start | bytes 6148
  740.1 271.6 %reduce-scatter.10.cloned.1.call-start = ((), (), s32[]{:S(2)}) async-start(), calls=%async_computation.11 | async-start | bytes 1572864 | tf_op jit(solution)/shard_map/reduce_scatter | solution.py:199
  740.8 148.5 %copy-start.71 = (f32[512]{0:T(512)S(1)}, f32[512]{0:T(512)}, u32[]{:S(2)}) copy-start(f32[512]{0:T(512)} %get-tuple-element.115) | copy-start | bytes 6148
  940.2 28.1 %copy-start.19 = (bf16[512,16,64]{0,2,1:T(8,128)(2,1)S(1)}, bf16[512,16,64]{0,2,1:T(8,128)(2,1)}, u32[]{:S(2)}) copy-start(bf16[512,16,64]{0,2,1:T(8,128)(2,1)} %copy-done.18) | copy-start | bytes 3145732
  990.5 127.8 %reduce-scatter.12.cloned.1.call-start = ((), (), s32[]{:S(2)}) async-start(), calls=%async_computation.12 | async-start | bytes 11796480 | tf_op jit(solution)/shard_map/reduce_scatter | solution.py:221
  1036.6 115.8 %reduce-scatter.14.cloned.1.call-start = ((), (), s32[]{:S(2)}) async-start(), calls=%async_computation.13 | async-start | bytes 1638400 | tf_op jit(solution)/shard_map/reduce_scatter | solution.py:232
  1120.9 242.8 %all-reduce.4.cloned.1.call-start = ((), (), s32[]{:S(2)}) async-start(), calls=%async_computation.17 | async-start | bytes 31457280 | tf_op jit(solution)/shard_map/psum | solution.py:191
  1137.8 17.9 %copy-start.80 = (f32[128]{0:T(128)S(1)}, f32[128]{0:T(128)}, u32[]{:S(2)}) copy-start(f32[128]{0:T(128)} %copy-done.79) | copy-start | bytes 1540
  1137.8 344.2 %all-gather.20.cloned.1.call-start = ((), (), s32[]{:S(2)}) async-start(), calls=%async_computation.14 | async-start | bytes 2359296 | tf_op jit(solution)/shard_map/all_gather | solution.py:233
  1154.1 335.8 %all-gather.24.cloned.1.call-start = ((), (), s32[]{:S(2)}) async-start(), calls=%async_computation.16 | async-start | bytes 2162688 | tf_op jit(solution)/shard_map/all_gather | solution.py:237
  1389.2 86.2 %copy-start.70 = (f32[512]{0:T(512)S(1)}, f32[512]{0:T(512)}, u32[]{:S(2)}) copy-start(f32[512]{0:T(512)} %get-tuple-element.113) | copy-start | bytes 6148
  (73 other events, 341.3 us)
Sparse Core Ops, SparseCore 0:
  17.3 23.9 all-gather.11
  44.9 62.0 all-gather.21
  110.4 60.5 all-gather.13
  180.1 148.1 all-gather.15
  379.0 143.7 reduce-scatter.5
  528.3 150.2 all-gather.17
  740.2 142.6 reduce-scatter.7
  990.6 21.0 reduce-scatter.9
  1036.7 81.5 reduce-scatter.11
  1121.1 31.1 reduce-scatter.13
  1157.4 206.2 all-reduce.3
  1366.0 28.3 all-gather.19
  1397.8 58.5 all-gather.23
where the time goes:
time: 1520 us
  waiting for transfers between devices  899 us (59%)
  matrix products  289 us (19%)
  other arithmetic  127 us (8%)
  blocking collectives  121 us (8%)
  local copies, waits for them, and re-layouts  61 us (4%)
  between operations  17.7 us (1%)
    psum x1, waiting for transfers between devices, body(): lax.psum(g.astype(BF), 'dp').astype(F32)  208 us
    all_gather x1, waiting for transfers between devices, body(): cot_all = lax.all_gather(cot.astype(BF), 'tensor', axis=0, tiled=True)  150 us
    all_gather x1, waiting for transfers between devices, body(): normed_two_all = lax.all_gather(normed_two, 'tensor', axis=0, tiled=True)  148 us
    reduce_scatter x1, waiting for transfers between devices, body(): lax.psum_scatter((dot_t(dgate, w_gate) + dot_t(dup, w_up)).astype(BF), 't...  142 us
    reduce_scatter x1, waiting for transfers between devices, body(): lax.psum_scatter(dot(hidden, w_down).astype(BF), 'tensor', scatter_dimens...  98.7 us
    all_gather x1, blocking collectives, sum_small(): lax.all_gather(vector[None], ('dp', 'tensor'), axis=0, tiled=True)  78 us
    dot_general x7, matrix products, dot_t(): lax.dot_general(a, b, (((1,), (1,)), ((), ())), preferred_element_type=F32)  74.9 us
    all_gather x1, waiting for transfers between devices, body(): lax.all_gather(query_cut, ('dp', 'tensor'), axis=0, tiled=False)  63.4 us
  transfers between devices with their start and end apart: 13, of which 11 were waited for; matrix products, arithmetic and copies ran while one was open for 12% of the time, Pallas kernels for 0%

commit v1 on v0

--- a/solution.py
+++ b/solution.py
@@ -188,7 +188,8 @@
     grad_gate = t_dot(normed_two_all, dgate)
     grad_up = t_dot(normed_two_all, dup)
     grad_gate, grad_up, grad_down = (
-        lax.psum(g.astype(BF), "dp").astype(F32) for g in (grad_gate, grad_up, grad_down)
+        jnp.sum(lax.all_gather(g.astype(BF), "dp"), axis=0).astype(F32)
+        for g in (grad_gate, grad_up, grad_down)
     )
     grad_ffn_gain = jnp.sum(dn2 * middle * factor_two, 0)
     dmiddle = cot + norm_back(dn2, middle, factor_two, ffn_gain)

time: 1520 us -> 1880 us (1.24)
  waiting for transfers between devices: 899 us -> 1190 us
  other arithmetic: 127 us -> 194 us
    all_gather x0 -> x3, waiting for transfers between devices: none -> 449 us  [body(): lax.all_gather(g.astype(BF), 'dp')]
    psum x1 -> x0, waiting for transfers between devices: 208 us -> none  [body(): lax.psum(g.astype(BF), 'dp').astype(F32)]
    reduce_sum x0 -> x3, other arithmetic: none -> 59.7 us  [body(): jnp.sum(lax.all_gather(g.astype(BF), 'dp'), axis=0).astype(F32)]
    reduce_scatter x1, waiting for transfers between devices: 47.8 us -> 81.7 us  [body(): wide = lax.psum_scatter(wide, 'dp', scatter_dimension=0, tiled=True)]
  transfers between devices with their start and end apart: 13 -> 15, of which waited for: 11 -> 13; matrix products, arithmetic and copies ran while one was open for 12% -> 13% of each run, Pallas kernels for 0% -> 0%
where the time goes in v1:
time: 1880 us
  waiting for transfers between devices  1190 us (63%)
  matrix products  292 us (16%)
  other arithmetic  194 us (10%)
  blocking collectives  121 us (6%)
  local copies, waits for them, and re-layouts  63 us (3%)
    all_gather x3, waiting for transfers between devices, body(): lax.all_gather(g.astype(BF), 'dp')  449 us
    all_gather x1, waiting for transfers between devices, body(): cot_all = lax.all_gather(cot.astype(BF), 'tensor', axis=0, tiled=True)  150 us
    all_gather x1, waiting for transfers between devices, body(): normed_two_all = lax.all_gather(normed_two, 'tensor', axis=0, tiled=True)  148 us
    reduce_scatter x1, waiting for transfers between devices, body(): lax.psum_scatter((dot_t(dgate, w_gate) + dot_t(dup, w_up)).astype(BF), 't...  142 us
    reduce_scatter x1, waiting for transfers between devices, body(): lax.psum_scatter(dot(hidden, w_down).astype(BF), 'tensor', scatter_dimens...  98.6 us
    reduce_scatter x1, waiting for transfers between devices, body(): wide = lax.psum_scatter(wide, 'dp', scatter_dimension=0, tiled=True)  81.7 us
    all_gather x1, blocking collectives, sum_small(): lax.all_gather(vector[None], ('dp', 'tensor'), axis=0, tiled=True)  78 us
    dot_general x7, matrix products, dot_t(): lax.dot_general(a, b, (((1,), (1,)), ((), ())), preferred_element_type=F32)  77.5 us
  transfers between devices with their start and end apart: 15, of which 13 were waited for; matrix products, arithmetic and copies ran while one was open for 13% of the time, Pallas kernels for 0%

profile of v1, /device:TPU:0, one launch (start us, length us, event | category | flops | bytes accessed | tf_op | source)
XLA Modules:
  0.0 1879.7 jit_solution(5902942262046025155)
XLA Ops:
  27.3 17.6 all-gather.18.cloned.1.call-done
  47.2 63.4 %all-gather.28.cloned.1.call-done = bf16[8192,256]{1,0:T(8,128)(2,1)} async-done(((bf16[256,256]{1,0:T(8,128)(2,1)}), bf16[8192,256]{1,0:T(8,128)(2,1)}) %all-gather.28.cloned.1.call-update) | async-done | bytes 4194320 | tf_op jit(solution)/shard_map/all_gather | solution.py:132
  183.7 148.3 %all-gather.22.cloned.1.call-done = bf16[2048,2048]{1,0:T(8,128)(2,1)} async-done(((bf16[512,2048]{1,0:T(8,128)(2,1)}), bf16[2048,2048]{1,0:T(8,128)(2,1)}) %all-gather.22.cloned.1.call-update) | async-done | bytes 8388624 | tf_op jit(solution)/shard_map/all_gather | solution.py:165
  348.7 17.3 multiply_convert_fusion.2
  384.6 43.0 %all-reduce = f32[32]{0:T(128)S(1)} all-reduce(f32[32]{0:T(128)S(1)} %dynamic-update-slice), channel_id=2, replica_groups=mesh['dp'=8,'tensor'=4] {'dp','tensor'}, use_global_device_ids=true, to_apply=%add | all-reduce | flops 32 | bytes 256
  427.7 98.6 %reduce-scatter.6.cloned.1.call-done = bf16[512,2048]{1,0:T(8,128)(2,1)} async-done(((bf16[2048,2048]{1,0:T(8,128)(2,1)}), bf16[512,2048]{1,0:T(8,128)(2,1)}) %reduce-scatter.6.cloned.1.call-update) | async-done | bytes 2097168 | tf_op jit(solution)/shard_map/reduce_scatter | solution.py:170
  531.9 150.5 %all-gather.24.cloned.1.call-done = bf16[2048,2048]{1,0:T(8,128)(2,1)} async-done(((bf16[512,2048]{1,0:T(8,128)(2,1)}), bf16[2048,2048]{1,0:T(8,128)(2,1)}) %all-gather.24.cloned.1.call-update) | async-done | bytes 8388624 | tf_op jit(solution)/shard_map/all_gather | solution.py:177
  682.3 24.3 %multiply_convert_fusion = (bf16[2048,1280]{1,0:T(8,128)(2,1)}, bf16[2048,1280]{1,0:T(8,128)(2,1)}) fusion(f32[2048,1280]{1,0:T(8,128)} %fusion.78, f32[2048,1280]{1,0:T(8,128)} %get-tuple-element.125, bf16[2048,2048]{1,0:T(8,128)(2,1)} %all-gather.24.cloned.1.call-done, bf16[1280,2048]{1,0:T(8,128)(2,1)} %param.29), kind=kOutput, calls=%fused_computation.17 | convolution fusion | flops 10771496960 | bytes 45088768 | tf_op jit(solution)/shard_map/dot_general | solution.py:51
  706.6 17.8 fusion.79
  724.4 19.4 %add_convert_fusion = bf16[2048,2048]{1,0:T(8,128)(2,1)} fusion(f32[2048,2048]{1,0:T(8,128)} %fusion.79, bf16[2048,1280]{1,0:T(8,128)(2,1)} %get-tuple-element.78, bf16[2048,1280]{1,0:T(8,128)(2,1)} %param.28), kind=kOutput, calls=%fused_computation.11 | convolution fusion | flops 10745806848 | bytes 35651584 | tf_op jit(solution)/shard_map/dot_general | solution.py:51
  744.6 142.1 %reduce-scatter.8.cloned.1.call-done = bf16[512,2048]{1,0:T(8,128)(2,1)} async-done(((bf16[2048,2048]{1,0:T(8,128)(2,1)}), bf16[512,2048]{1,0:T(8,128)(2,1)}) %reduce-scatter.8.cloned.1.call-update) | async-done | bytes 2097168 | tf_op jit(solution)/shard_map/reduce_scatter | solution.py:182
  919.5 24.5 %fusion = (f32[4,4,512]{2,1,0:T(4,128)S(1)}, f32[4,1024,512,4]{2,1,3,0:T(8,128)}) fusion(f32[4,4,512]{2,1,0:T(4,128)S(1)} %bitcast.238, pred[512,1024]{0,1:T(8,128)(4,1)S(1)} %copy-done.10, f32[4,1024,512,4]{2,1,3,0:T(8,128)} %get-tuple-element.121, bf16[1024,4,64,1]{0,2,3,1:T(8,128)(2,1)S(1)} %bitcast.234, bf16[512,4,4,64]{0,3,2,1:T(8,128)(2,1)S(1)} %bitcast.232), kind=kOutput, calls=%fused_computation.2 | convolution fusion | flops 1124065280 | bytes 69271552 | tf_op jit(solution)/shard_map/ikgd,jkd->kgij/dot_general | solution.py:88
  944.0 28.1 %fusion.2 = bf16[4,4,512,1024]{2,3,1,0:T(8,128)(2,1)} fusion(f32[4,1024,512,4]{2,1,3,0:T(8,128)} %get-tuple-element.127, f32[4,4,512]{2,1,0:T(4,128)S(1)} %get-tuple-element.126, f32[4,4,512]{2,1,0:T(4,128)S(1)} %bitcast.239, pred[512,1024]{0,1:T(8,128)(4,1)S(1)} %copy-done.10, f32[4,1024,512,4]{2,1,3,0:T(8,128)} %get-tuple-element.121), kind=kLoop, calls=%fused_computation.4 | loop fusion | flops 58720256 | bytes 84475904 | tf_op jit(solution)/shard_map/convert_element_type | solution.py:90
  1022.5 18.0 pad_maximum_fusion
  1040.6 81.7 %reduce-scatter.12.cloned.1.call-done = bf16[256,2560]{0,1:T(8,128)(2,1)} async-done(((bf16[2048,2560]{0,1:T(8,128)(2,1)}), bf16[256,2560]{0,1:T(8,128)(2,1)}) %reduce-scatter.12.cloned.1.call-update) | async-done | bytes 1310736 | tf_op jit(solution)/shard_map/reduce_scatter | solution.py:222
  1124.9 31.4 %reduce-scatter.14.cloned.1.call-done = bf16[256,640]{0,1:T(8,128)(2,1)} async-done(((bf16[256,2560]{0,1:T(8,128)(2,1)}), bf16[256,640]{0,1:T(8,128)(2,1)}) %reduce-scatter.14.cloned.1.call-update) | async-done | bytes 327696 | tf_op jit(solution)/shard_map/reduce_scatter | solution.py:233
  1176.8 16.7 convolution_convert_fusion.2
  1225.3 78.0 %all-gather.6 = f32[32,1,4352]{2,1,0:T(1,128)} all-gather(f32[1,1,4352]{2,1,0:T(1,128)S(1)} %reshape.253), channel_id=4, replica_groups=mesh['dp'=8,'tensor'=4] {'dp','tensor'}, dimensions={0}, use_global_device_ids=true | all-gather | bytes 574464 | tf_op jit(solution)/shard_map/all_gather | solution.py:98
  1340.5 107.4 %all-gather.32.cloned.1.call-done = bf16[16384,1280]{1,0:T(8,128)(2,1)} async-done(((bf16[2048,1280]{1,0:T(8,128)(2,1)}), bf16[16384,1280]{1,0:T(8,128)(2,1)}) %all-gather.32.cloned.1.call-update) | async-done | bytes 41943056 | tf_op jit(solution)/shard_map/all_gather | solution.py:191
  1447.9 21.1 %reduce_sum.225 = bf16[2048,1280]{1,0:T(8,128)(2,1)} reduce(bf16[8,2048,1280]{2,1,0:T(8,128)(2,1)} %bitcast.207, bf16[]{:T(256)} %constant.87.clone.1), dimensions={0}, to_apply=%region_25.26 | reduce | flops 18350080 | bytes 47185920 | tf_op jit(solution)/shard_map/reduce_sum | solution.py:191
  1476.3 171.2 %all-gather.34.cloned.1.call-done = bf16[16384,1280]{1,0:T(8,128)(2,1)} async-done(((bf16[2048,1280]{1,0:T(8,128)(2,1)}), bf16[16384,1280]{1,0:T(8,128)(2,1)}) %all-gather.34.cloned.1.call-update) | async-done | bytes 41943056 | tf_op jit(solution)/shard_map/all_gather | solution.py:191
  1647.5 21.4 %reduce_sum.226 = bf16[2048,1280]{1,0:T(8,128)(2,1)} reduce(bf16[8,2048,1280]{2,1,0:T(8,128)(2,1)} %bitcast.208, bf16[]{:T(256)} %constant.87.clone.1), dimensions={0}, to_apply=%region_26.27 | reduce | flops 18350080 | bytes 47185920 | tf_op jit(solution)/shard_map/reduce_sum | solution.py:191
  1676.3 170.3 %all-gather.36.cloned.1.call-done = bf16[10240,2048]{1,0:T(8,128)(2,1)} async-done(((bf16[1280,2048]{1,0:T(8,128)(2,1)}), bf16[10240,2048]{1,0:T(8,128)(2,1)}) %all-gather.36.cloned.1.call-update) | async-done | bytes 41943056 | tf_op jit(solution)/shard_map/all_gather | solution.py:191
  1846.6 17.2 reduce_sum.227
  (288 shorter events, 332.8 us)
Async XLA Ops:
  7.2 37.7 %all-gather.18.cloned.1.call-start = ((), (), s32[]{:S(2)}) async-start(), calls=%async_computation.5 | async-start | bytes 1572864 | tf_op jit(solution)/shard_map/all_gather | solution.py:148
  10.1 112.2 %copy-start.57 = (f32[512]{0:T(512)}, f32[512]{0:T(512)S(1)}, u32[]{:S(2)}) copy-start(f32[512]{0:T(512)S(1)} %get-tuple-element.111) | copy-start | bytes 6148
  16.2 102.4 %copy-start.61 = (f32[256]{0:T(256)}, f32[256]{0:T(256)S(1)}, u32[]{:S(2)}) copy-start(f32[256]{0:T(256)S(1)} %mul.446) | copy-start | bytes 3076
  16.5 109.8 %copy-start.26 = (f32[512,64]{0,1:T(8,128)}, f32[512,64]{0,1:T(8,128)S(1)}, u32[]{:S(2)}) copy-start(f32[512,64]{0,1:T(8,128)S(1)} %get-tuple-element.129) | copy-start | bytes 393220
  16.5 109.8 %copy-start.31 = (f32[512,64]{0,1:T(8,128)}, f32[512,64]{0,1:T(8,128)S(1)}, u32[]{:S(2)}) copy-start(f32[512,64]{0,1:T(8,128)S(1)} %get-tuple-element.130) | copy-start | bytes 393220
  20.7 89.9 %all-gather.28.cloned.1.call-start = ((), (), s32[]{:S(2)}) async-start(), calls=%async_computation.15 | async-start | bytes 4325376 | tf_op jit(solution)/shard_map/all_gather | solution.py:132
  22.4 152.3 %all-gather.20.cloned.1.call-start = ((), (), s32[]{:S(2)}) async-start(), calls=%async_computation.6 | async-start | bytes 4325376 | tf_op jit(solution)/shard_map/all_gather | solution.py:139
  24.0 308.0 %all-gather.22.cloned.1.call-start = ((), (), s32[]{:S(2)}) async-start(), calls=%async_computation.7 | async-start | bytes 10485760 | tf_op jit(solution)/shard_map/all_gather | solution.py:165
  183.6 342.8 %reduce-scatter.6.cloned.1.call-start = ((), (), s32[]{:S(2)}) async-start(), calls=%async_computation.8 | async-start | bytes 10485760 | tf_op jit(solution)/shard_map/reduce_scatter | solution.py:170
  382.5 143.9 %copy-start.12 = (bf16[512,2048]{1,0:T(8,128)(2,1)S(1)}, bf16[512,2048]{1,0:T(8,128)(2,1)}, u32[]{:S(2)}) copy-start(bf16[512,2048]{1,0:T(8,128)(2,1)} %param.16) | copy-start | bytes 6291460
  382.5 299.8 %all-gather.24.cloned.1.call-start = ((), (), s32[]{:S(2)}) async-start(), calls=%async_computation.9 | async-start | bytes 10485760 | tf_op jit(solution)/shard_map/all_gather | solution.py:177
  427.6 104.1 %copy-start.74 = (f32[128]{0:T(128)}, f32[128]{0:T(128)S(1)}, u32[]{:S(2)}) copy-start(f32[128]{0:T(128)S(1)} %broadcast_reduce_fusion) | copy-start | bytes 1540
  531.8 354.9 %reduce-scatter.8.cloned.1.call-start = ((), (), s32[]{:S(2)}) async-start(), calls=%async_computation.10 | async-start | bytes 10485760 | tf_op jit(solution)/shard_map/reduce_scatter | solution.py:182
  743.8 142.9 %copy-start.50 = (f32[2048]{0:T(1024)S(1)}, f32[2048]{0:T(1024)}, u32[]{:S(2)}) copy-start(f32[2048]{0:T(1024)} %param.26) | copy-start | bytes 24580
  743.8 142.9 %copy-start.56 = (f32[512]{0:T(512)S(1)}, f32[512]{0:T(512)}, u32[]{:S(2)}) copy-start(f32[512]{0:T(512)} %copy-done.55) | copy-start | bytes 6148
  743.9 271.7 %reduce-scatter.10.cloned.1.call-start = ((), (), s32[]{:S(2)}) async-start(), calls=%async_computation.11 | async-start | bytes 1572864 | tf_op jit(solution)/shard_map/reduce_scatter | solution.py:200
  744.6 148.6 %copy-start.66 = (f32[512]{0:T(512)S(1)}, f32[512]{0:T(512)}, u32[]{:S(2)}) copy-start(f32[512]{0:T(512)} %get-tuple-element.112) | copy-start | bytes 6148
  994.4 127.8 %reduce-scatter.12.cloned.1.call-start = ((), (), s32[]{:S(2)}) async-start(), calls=%async_computation.12 | async-start | bytes 11796480 | tf_op jit(solution)/shard_map/reduce_scatter | solution.py:222
  1040.5 115.8 %reduce-scatter.14.cloned.1.call-start = ((), (), s32[]{:S(2)}) async-start(), calls=%async_computation.13 | async-start | bytes 1638400 | tf_op jit(solution)/shard_map/reduce_scatter | solution.py:233
  1124.8 188.7 %all-gather.26.cloned.1.call-start = ((), (), s32[]{:S(2)}) async-start(), calls=%async_computation.14 | async-start | bytes 2359296 | tf_op jit(solution)/shard_map/all_gather | solution.py:234
  1158.0 163.4 %all-gather.30.cloned.1.call-start = ((), (), s32[]{:S(2)}) async-start(), calls=%async_computation.16 | async-start | bytes 2162688 | tf_op jit(solution)/shard_map/all_gather | solution.py:238
  1159.9 287.9 %all-gather.32.cloned.1.call-start = ((), (), s32[]{:S(2)}) async-start(), calls=%async_computation.17 | async-start | bytes 47185920 | tf_op jit(solution)/shard_map/all_gather | solution.py:191
  1176.7 470.8 %all-gather.34.cloned.1.call-start = ((), (), s32[]{:S(2)}) async-start(), calls=%async_computation.18 | async-start | bytes 47185920 | tf_op jit(solution)/shard_map/all_gather | solution.py:191
  1193.5 653.1 %all-gather.36.cloned.1.call-start = ((), (), s32[]{:S(2)}) async-start(), calls=%async_computation.19 | async-start | bytes 47185920 | tf_op jit(solution)/shard_map/all_gather | solution.py:191
  (68 other events, 463.1 us)
Sparse Core Ops, SparseCore 0:
  20.9 24.0 all-gather.17
  48.5 62.0 all-gather.27
  114.0 60.5 all-gather.19
  183.7 148.2 all-gather.21
  382.6 143.7 reduce-scatter.5
  531.9 150.3 all-gather.23
  744.0 142.6 reduce-scatter.7
  994.5 21.0 reduce-scatter.9
  1040.6 81.5 reduce-scatter.11
  1125.1 31.1 reduce-scatter.13
  1158.9 26.9 all-gather.25
  1189.6 58.7 all-gather.29
  1251.1 196.7 all-gather.31
  1450.4 197.1 all-gather.33
  1649.4 197.1 all-gather.35
